TPU v7x, 128 devices: a whole 4x4x4 slice. The times are simulated.
128 devices in a mesh: wide: 16 (over y_lo, z, core), narrow: 8 (over x, y_hi).
Axes of the slice: x: 4, y: 4 (y_hi: 2, y_lo: 2; y = y_hi * 2 + y_lo), z: 4, core: 2. Of those that a mesh axis runs over, the one named last changes fastest.
Arguments:
- fields: float32 [5, 16, 64, 256], P(None, 'wide', 'narrow'), may hold values from -2.1 to 6.1, as said below
- prior_modes: bfloat16 [124, 5, 16, 16384], P(None, None, 'wide', 'narrow'), may hold values from -360 to 360, as said below
Outputs:
- flow_state: float32 [5, 16, 64, 256], P(None, 'wide', 'narrow')
- factor: float32 [128, 128], replicated
Inputs may be any that keep to these rules, and one draw needn't show every extreme that they name: `fields`: density and pressure lie in 0.6 to 1.4, each velocity component below 1.5 in magnitude. `prior_modes`: the columns are linearly independent.
All inputs are finite; a program needn't handle non-finite values.
Results may differ from a plain program's by a relative error of at most 0.0014.
Values may be sent and summed in bfloat16 or wider, within the bound.
No kernel may reach another device: no remote copies, remote signals or barrier semaphores. Data moves between devices by JAX's collectives and lax.ppermute only.
A program may use at most 64 MiB of HBM per device.

v0:
```python
import jax
import jax.numpy as jnp
from jax import lax
from jax.sharding import PartitionSpec as P

STEPS = 2
GAMMA = 1.4
TIME_STEP = 0.25
VISCOSITY = 0.15


def extended(block, sides, width):
    for axis, dim in sides:
        count = lax.axis_size(axis)
        forward = [(i, i + 1) for i in range(count - 1)]
        forward.append((count - 1, 0))
        backward = [(target, source) for source, target in forward]
        low = lax.ppermute(
            lax.slice_in_dim(block, block.shape[dim] - width, None, axis=dim), axis, forward
        )
        high = lax.ppermute(lax.slice_in_dim(block, 0, width, axis=dim), axis, backward)
        block = jnp.concatenate([low, block, high], axis=dim)
    return block


def flux_of(current, dim_index):
    density = current[0]
    momentum = current[1:4]
    energy = current[4]
    vel_d = momentum[dim_index] / density
    pressure = (GAMMA - 1.0) * (
        energy
        - 0.5
        * (momentum[0] * momentum[0] + momentum[1] * momentum[1] + momentum[2] * momentum[2])
        / density
    )
    components = [
        momentum[dim_index],
        momentum[0] * vel_d,
        momentum[1] * vel_d,
        momentum[2] * vel_d,
        (energy + pressure) * vel_d,
    ]
    components[1 + dim_index] = components[1 + dim_index] + pressure
    return jnp.stack(components)


def tendency(current):
    padded = extended(current.astype(jnp.bfloat16), (("wide", 1), ("narrow", 2)), 1).astype(
        current.dtype
    )
    flux_x = flux_of(padded[:, :, 1:-1], 0)
    flux_y = flux_of(padded[:, 1:-1, :], 1)
    flux_z = flux_of(current, 2)
    divergence = (
        flux_x[:, 2:]
        - flux_x[:, :-2]
        + (flux_y[:, :, 2:] - flux_y[:, :, :-2])
        + (jnp.roll(flux_z, -1, 3) - jnp.roll(flux_z, 1, 3))
    )
    laplace = (
        padded[:, 2:, 1:-1]
        + padded[:, :-2, 1:-1]
        + padded[:, 1:-1, 2:]
        + padded[:, 1:-1, :-2]
        + jnp.roll(current, -1, 3)
        + jnp.roll(current, 1, 3)
        - 6.0 * current
    )
    return -0.5 * divergence + VISCOSITY * laplace


def local(fields, prior_modes):
    wide_count = lax.axis_size("wide")
    narrow_count = lax.axis_size("narrow")
    cells_x, cells_y, cells_z = (fields.shape[1], fields.shape[2], fields.shape[3])
    inverse_cells = 1.0 / (cells_x * wide_count * cells_y * narrow_count * cells_z)
    flat_modes = prior_modes.reshape(prior_modes.shape[0], -1)
    contract = (((1,), (1,)), ((), ()))
    gram_modes = lax.dot_general(
        flat_modes, flat_modes, contract, preferred_element_type=jnp.float32
    )
    current = fields
    snapshots = []
    for step_index in range(STEPS):
        section_one = current + TIME_STEP * tendency(current)
        snapshots.append(section_one.astype(jnp.bfloat16))
        current = 0.5 * current + 0.5 * (section_one + TIME_STEP * tendency(section_one))
        snapshots.append(current.astype(jnp.bfloat16))
    arrived = lax.all_to_all(
        jnp.stack(snapshots), "narrow", split_axis=4, concat_axis=3, tiled=True
    )
    snap_rows = jnp.swapaxes(arrived, 3, 4).reshape(arrived.shape[0], -1)
    cross_gram = lax.dot_general(
        flat_modes, snap_rows, contract, preferred_element_type=jnp.float32
    )
    snap_gram = lax.dot_general(snap_rows, snap_rows, contract, preferred_element_type=jnp.float32)
    gram_local = jnp.concatenate(
        [
            jnp.concatenate([gram_modes, cross_gram], 1),
            jnp.concatenate([cross_gram.T, snap_gram], 1),
        ],
        0,
    )
    gram_local = gram_local * inverse_cells
    gram_whole = lax.psum(gram_local, ("wide", "narrow"))
    factor = jnp.linalg.cholesky(gram_whole).T
    return (current, factor)


def solution(mesh):
    placed = (P(None, "wide", "narrow", None), P(None, None, "wide", "narrow"))
    return jax.shard_map(
        local,
        mesh=mesh,
        in_specs=placed,
        out_specs=(P(None, "wide", "narrow", None), P()),
        check_vma=False,
    )
```

profile of v0, /device:TPU:1, one launch (start us, length us, event | category | flops | bytes accessed | tf_op | source)
XLA Modules:
  0.0 256.1 jit_solution(13830206497082720852)
XLA Ops:
  7.9 1.4 collective-permute-start.1
  9.3 1.6 collective-permute-start
  15.7 5.2 %collective-permute-start.3 = (bf16[5,3,1,256]{3,1,2,0:T(4,128)(2,1)S(1)}, bf16[5,3,1,256]{3,1,2,0:T(4,128)(2,1)S(1)}, u32[]{:S(2)}, u32[]{:S(2)}) collective-permute-start(bf16[5,3,1,256]{3,1,2,0:T(4,128)(2,1)S(1)} %copy.427), channel_id=1, source_target_pairs={{1,0},{2,1},{3,2},{4,3},{5,4},{6,5},{7,6},{0,7},{9,8},{10,9},{11,1... | collective-permute-start | bytes 23048 | tf_op jit(solution)/shard_map/ppermute | solution.py:21
  21.7 5.3 %collective-permute-done.2 = bf16[5,3,1,256]{3,1,2,0:T(4,128)(2,1)S(1)} collective-permute-done((bf16[5,3,1,256]{3,1,2,0:T(4,128)(2,1)S(1)}, bf16[5,3,1,256]{3,1,2,0:T(4,128)(2,1)S(1)}, u32[]{:S(2)}, u32[]{:S(2)}) %collective-permute-start.2) | collective-permute-done | bytes 7712 | tf_op jit(solution)/shard_map/ppermute | solution.py:18
  28.2 4.9 %collective-permute-start.5 = (bf16[5,1,8,256]{3,2,0,1:T(8,128)(2,1)S(1)}, bf16[5,1,8,256]{3,2,0,1:T(8,128)(2,1)S(1)}, u32[]{:S(2)}, u32[]{:S(2)}) collective-permute-start(bf16[5,1,8,256]{3,2,0,1:T(8,128)(2,1)S(1)} %get-tuple-element.65), channel_id=1, source_target_pairs={{8,0},{16,8},{24,16},{32,24},{40,32},{48,40},{56,48},{64,56},{72,6... | collective-permute-start | bytes 61448 | tf_op jit(solution)/shard_map/ppermute | solution.py:21
  35.6 2.3 collective-permute-start.6
  38.0 1.1 collective-permute-done.7
  39.1 2.6 %collective-permute-done.6 = bf16[5,3,1,256]{3,1,2,0:T(4,128)(2,1)S(1)} collective-permute-done((bf16[5,3,1,256]{3,1,2,0:T(4,128)(2,1)S(1)}, bf16[5,3,1,256]{3,1,2,0:T(4,128)(2,1)S(1)}, u32[]{:S(2)}, u32[]{:S(2)}) %collective-permute-start.6) | collective-permute-done | bytes 7712 | tf_op jit(solution)/shard_map/ppermute | solution.py:18
  42.3 6.1 %collective-permute-start.9 = (bf16[5,1,8,256]{3,2,0,1:T(8,128)(2,1)S(1)}, bf16[5,1,8,256]{3,2,0,1:T(8,128)(2,1)S(1)}, u32[]{:S(2)}, u32[]{:S(2)}) collective-permute-start(bf16[5,1,8,256]{3,2,0,1:T(8,128)(2,1)S(1)} %fusion.78), channel_id=1, source_target_pairs={{8,0},{16,8},{24,16},{32,24},{40,32},{48,40},{56,48},{64,56},{72,6... | collective-permute-start | bytes 61448 | tf_op jit(solution)/shard_map/ppermute | solution.py:21
  49.8 2.9 %collective-permute-start.10 = (bf16[5,3,1,256]{3,1,2,0:T(4,128)(2,1)S(1)}, bf16[5,3,1,256]{3,1,2,0:T(4,128)(2,1)S(1)}, u32[]{:S(2)}, u32[]{:S(2)}) collective-permute-start(bf16[5,3,1,256]{3,1,2,0:T(4,128)(2,1)S(1)} %copy.394), channel_id=1, source_target_pairs={{0,1},{1,2},{2,3},{3,4},{4,5},{5,6},{6,7},{7,0},{8,9},{9,10},{10,1... | collective-permute-start | bytes 23048 | tf_op jit(solution)/shard_map/ppermute | solution.py:18
  52.8 1.0 collective-permute-done.11
  53.8 2.2 collective-permute-done.10
  56.4 5.4 %collective-permute-start.13 = (bf16[5,1,8,256]{3,2,0,1:T(8,128)(2,1)S(1)}, bf16[5,1,8,256]{3,2,0,1:T(8,128)(2,1)S(1)}, u32[]{:S(2)}, u32[]{:S(2)}) collective-permute-start(bf16[5,1,8,256]{3,2,0,1:T(8,128)(2,1)S(1)} %get-tuple-element.31), channel_id=1, source_target_pairs={{8,0},{16,8},{24,16},{32,24},{40,32},{48,40},{56,48},{64,56},{72,6... | collective-permute-start | bytes 61448 | tf_op jit(solution)/shard_map/ppermute | solution.py:21
  63.2 2.9 %collective-permute-start.14 = (bf16[5,3,1,256]{3,1,2,0:T(4,128)(2,1)S(1)}, bf16[5,3,1,256]{3,1,2,0:T(4,128)(2,1)S(1)}, u32[]{:S(2)}, u32[]{:S(2)}) collective-permute-start(bf16[5,3,1,256]{3,1,2,0:T(4,128)(2,1)S(1)} %copy.405), channel_id=1, source_target_pairs={{0,1},{1,2},{2,3},{3,4},{4,5},{5,6},{6,7},{7,0},{8,9},{9,10},{10,1... | collective-permute-start | bytes 23048 | tf_op jit(solution)/shard_map/ppermute | solution.py:18
  66.2 1.0 collective-permute-done.15
  67.2 2.2 collective-permute-done.14
  71.2 2.1 reshape.630
  73.3 3.4 %all-to-all-start = ((bf16[8,2,2560]{2,1,0:T(2,128)(2,1)}), bf16[8,2,2560]{2,1,0:T(2,128)(2,1)S(1)}, u32[]{:S(2)}, u32[]{:S(2)}) async-start(bf16[8,2,2560]{2,1,0:T(2,128)(2,1)} %reshape.630), calls=%async_computation | async-start | bytes 163840 | tf_op jit(solution)/shard_map/all_to_all | solution.py:90
  76.9 3.4 %fusion.2 = f32[124,124]{0,1:T(8,128)S(1)} fusion(bf16[124,5,1,2048]{3,0,2,1:T(8,128)(2,1)} %param.3), kind=kOutput, calls=%fused_computation.2 | convolution fusion | flops 314900480 | bytes 2601024 | tf_op jit(solution)/shard_map/dot_general | solution.py:80
  80.2 3.3 %copy.420 = bf16[124,5,1,2048]{0,3,1,2:T(8,128)(2,1)S(1)} copy(bf16[124,5,1,2048]{3,0,2,1:T(8,128)(2,1)} %param.3) | data formatting | bytes 5079040 | tf_op args[1]
  83.6 2.6 %reshape.631 = bf16[256,5,1,4,8]{4,3,2,1,0:T(4,128)(2,1)} reshape(bf16[8,2,2560]{2,1,0:T(2,128)(2,1)S(1)} %all-to-all-done) | data formatting | bytes 163840
  86.2 1.8 copy.417
  90.1 143.6 %all-reduce.2.cloned.1.call-done = f32[128,128]{0,1:T(8,128)} async-done(((f32[128,128]{0,1:T(8,128)}), f32[128,128]{0,1:T(8,128)}) %all-reduce.2.cloned.1.call-update) | async-done | bytes 65552 | tf_op jit(solution)/shard_map/psum | solution.py:106
  235.5 11.7 %cholesky.18 = f32[128,128]{1,0:T(8,128)S(1)} custom-call(f32[128,128]{1,0:T(8,128)S(1)} %fusion.6), custom_call_target="Cholesky" | custom-call | tf_op jit(solution)/shard_map/jit(cholesky)/cholesky | solution.py:107
  (143 shorter events, 21.4 us)
Async XLA Ops:
  7.9 7.6 %collective-permute-start.1 = (bf16[5,1,8,256]{3,2,1,0:T(8,128)(2,1)S(1)}, bf16[5,1,8,256]{3,2,1,0:T(8,128)(2,1)S(1)}, u32[]{:S(2)}, u32[]{:S(2)}) collective-permute-start(bf16[5,1,8,256]{3,2,1,0:T(8,128)(2,1)S(1)} %convert_element_type.30), channel_id=1, source_target_pairs={{8,0},{16,8},{24,16},{32,24},{40,32},{48,40},{56,48},{64,56},{72,6... | collective-permute-start | bytes 61448 | tf_op jit(solution)/shard_map/ppermute | solution.py:21
  9.3 6.3 %collective-permute-start = (bf16[5,1,8,256]{3,2,1,0:T(8,128)(2,1)S(1)}, bf16[5,1,8,256]{3,2,1,0:T(8,128)(2,1)S(1)}, u32[]{:S(2)}, u32[]{:S(2)}) collective-permute-start(bf16[5,1,8,256]{3,2,1,0:T(8,128)(2,1)S(1)} %convert_element_type.30), channel_id=1, source_target_pairs={{0,8},{8,16},{16,24},{24,32},{32,40},{40,48},{48,56},{56,64},{64,7... | collective-permute-start | bytes 61448 | tf_op jit(solution)/shard_map/ppermute | solution.py:18
  11.7 30.4 %copy-start = (f32[5,1,8,256]{3,2,1,0:T(8,128)S(1)}, f32[5,1,8,256]{3,2,1,0:T(8,128)}, u32[]{:S(2)}) copy-start(f32[5,1,8,256]{3,2,1,0:T(8,128)} %param.2) | copy-start | bytes 122884
  15.7 6.0 %collective-permute-start.3 = (bf16[5,3,1,256]{3,1,2,0:T(4,128)(2,1)S(1)}, bf16[5,3,1,256]{3,1,2,0:T(4,128)(2,1)S(1)}, u32[]{:S(2)}, u32[]{:S(2)}) collective-permute-start(bf16[5,3,1,256]{3,1,2,0:T(4,128)(2,1)S(1)} %copy.427), channel_id=1, source_target_pairs={{1,0},{2,1},{3,2},{4,3},{5,4},{6,5},{7,6},{0,7},{9,8},{10,9},{11,1... | collective-permute-start | bytes 23048 | tf_op jit(solution)/shard_map/ppermute | solution.py:21
  20.8 6.1 %collective-permute-start.2 = (bf16[5,3,1,256]{3,1,2,0:T(4,128)(2,1)S(1)}, bf16[5,3,1,256]{3,1,2,0:T(4,128)(2,1)S(1)}, u32[]{:S(2)}, u32[]{:S(2)}) collective-permute-start(bf16[5,3,1,256]{3,1,2,0:T(4,128)(2,1)S(1)} %copy.426), channel_id=1, source_target_pairs={{0,1},{1,2},{2,3},{3,4},{4,5},{5,6},{6,7},{7,0},{8,9},{9,10},{10,1... | collective-permute-start | bytes 23048 | tf_op jit(solution)/shard_map/ppermute | solution.py:18
  28.2 5.7 %collective-permute-start.5 = (bf16[5,1,8,256]{3,2,0,1:T(8,128)(2,1)S(1)}, bf16[5,1,8,256]{3,2,0,1:T(8,128)(2,1)S(1)}, u32[]{:S(2)}, u32[]{:S(2)}) collective-permute-start(bf16[5,1,8,256]{3,2,0,1:T(8,128)(2,1)S(1)} %get-tuple-element.65), channel_id=1, source_target_pairs={{8,0},{16,8},{24,16},{32,24},{40,32},{48,40},{56,48},{64,56},{72,6... | collective-permute-start | bytes 61448 | tf_op jit(solution)/shard_map/ppermute | solution.py:21
  33.0 1.8 collective-permute-start.4
  34.9 4.2 %collective-permute-start.7 = (bf16[5,3,1,256]{3,1,2,0:T(4,128)(2,1)S(1)}, bf16[5,3,1,256]{3,1,2,0:T(4,128)(2,1)S(1)}, u32[]{:S(2)}, u32[]{:S(2)}) collective-permute-start(bf16[5,3,1,256]{3,1,2,0:T(4,128)(2,1)S(1)} %copy.383), channel_id=1, source_target_pairs={{1,0},{2,1},{3,2},{4,3},{5,4},{6,5},{7,6},{0,7},{9,8},{10,9},{11,1... | collective-permute-start | bytes 23048 | tf_op jit(solution)/shard_map/ppermute | solution.py:21
  35.6 6.1 %collective-permute-start.6 = (bf16[5,3,1,256]{3,1,2,0:T(4,128)(2,1)S(1)}, bf16[5,3,1,256]{3,1,2,0:T(4,128)(2,1)S(1)}, u32[]{:S(2)}, u32[]{:S(2)}) collective-permute-start(bf16[5,3,1,256]{3,1,2,0:T(4,128)(2,1)S(1)} %copy.382), channel_id=1, source_target_pairs={{0,1},{1,2},{2,3},{3,4},{4,5},{5,6},{6,7},{7,0},{8,9},{9,10},{10,1... | collective-permute-start | bytes 23048 | tf_op jit(solution)/shard_map/ppermute | solution.py:18
  42.3 7.0 %collective-permute-start.9 = (bf16[5,1,8,256]{3,2,0,1:T(8,128)(2,1)S(1)}, bf16[5,1,8,256]{3,2,0,1:T(8,128)(2,1)S(1)}, u32[]{:S(2)}, u32[]{:S(2)}) collective-permute-start(bf16[5,1,8,256]{3,2,0,1:T(8,128)(2,1)S(1)} %fusion.78), channel_id=1, source_target_pairs={{8,0},{16,8},{24,16},{32,24},{40,32},{48,40},{56,48},{64,56},{72,6... | collective-permute-start | bytes 61448 | tf_op jit(solution)/shard_map/ppermute | solution.py:21
  48.5 1.2 collective-permute-start.8
  49.7 4.1 %collective-permute-start.11 = (bf16[5,3,1,256]{3,1,2,0:T(4,128)(2,1)S(1)}, bf16[5,3,1,256]{3,1,2,0:T(4,128)(2,1)S(1)}, u32[]{:S(2)}, u32[]{:S(2)}) collective-permute-start(bf16[5,3,1,256]{3,1,2,0:T(4,128)(2,1)S(1)} %copy.395), channel_id=1, source_target_pairs={{1,0},{2,1},{3,2},{4,3},{5,4},{6,5},{7,6},{0,7},{9,8},{10,9},{11,1... | collective-permute-start | bytes 23048 | tf_op jit(solution)/shard_map/ppermute | solution.py:21
  49.8 6.2 %collective-permute-start.10 = (bf16[5,3,1,256]{3,1,2,0:T(4,128)(2,1)S(1)}, bf16[5,3,1,256]{3,1,2,0:T(4,128)(2,1)S(1)}, u32[]{:S(2)}, u32[]{:S(2)}) collective-permute-start(bf16[5,3,1,256]{3,1,2,0:T(4,128)(2,1)S(1)} %copy.394), channel_id=1, source_target_pairs={{0,1},{1,2},{2,3},{3,4},{4,5},{5,6},{6,7},{7,0},{8,9},{9,10},{10,1... | collective-permute-start | bytes 23048 | tf_op jit(solution)/shard_map/ppermute | solution.py:18
  56.4 6.3 %collective-permute-start.13 = (bf16[5,1,8,256]{3,2,0,1:T(8,128)(2,1)S(1)}, bf16[5,1,8,256]{3,2,0,1:T(8,128)(2,1)S(1)}, u32[]{:S(2)}, u32[]{:S(2)}) collective-permute-start(bf16[5,1,8,256]{3,2,0,1:T(8,128)(2,1)S(1)} %get-tuple-element.31), channel_id=1, source_target_pairs={{8,0},{16,8},{24,16},{32,24},{40,32},{48,40},{56,48},{64,56},{72,6... | collective-permute-start | bytes 61448 | tf_op jit(solution)/shard_map/ppermute | solution.py:21
  61.9 1.2 collective-permute-start.12
  63.1 4.1 %collective-permute-start.15 = (bf16[5,3,1,256]{3,1,2,0:T(4,128)(2,1)S(1)}, bf16[5,3,1,256]{3,1,2,0:T(4,128)(2,1)S(1)}, u32[]{:S(2)}, u32[]{:S(2)}) collective-permute-start(bf16[5,3,1,256]{3,1,2,0:T(4,128)(2,1)S(1)} %copy.406), channel_id=1, source_target_pairs={{1,0},{2,1},{3,2},{4,3},{5,4},{6,5},{7,6},{0,7},{9,8},{10,9},{11,1... | collective-permute-start | bytes 23048 | tf_op jit(solution)/shard_map/ppermute | solution.py:21
  63.2 6.2 %collective-permute-start.14 = (bf16[5,3,1,256]{3,1,2,0:T(4,128)(2,1)S(1)}, bf16[5,3,1,256]{3,1,2,0:T(4,128)(2,1)S(1)}, u32[]{:S(2)}, u32[]{:S(2)}) collective-permute-start(bf16[5,3,1,256]{3,1,2,0:T(4,128)(2,1)S(1)} %copy.405), channel_id=1, source_target_pairs={{0,1},{1,2},{2,3},{3,4},{4,5},{5,6},{6,7},{7,0},{8,9},{9,10},{10,1... | collective-permute-start | bytes 23048 | tf_op jit(solution)/shard_map/ppermute | solution.py:18
  73.3 10.3 %all-to-all-start = ((bf16[8,2,2560]{2,1,0:T(2,128)(2,1)}), bf16[8,2,2560]{2,1,0:T(2,128)(2,1)S(1)}, u32[]{:S(2)}, u32[]{:S(2)}) async-start(bf16[8,2,2560]{2,1,0:T(2,128)(2,1)} %reshape.630), calls=%async_computation | async-start | bytes 163840 | tf_op jit(solution)/shard_map/all_to_all | solution.py:90
  76.6 157.1 %all-reduce.2.cloned.1.call-start = ((), (), s32[]{:S(2)}) async-start(), calls=%async_computation.1 | async-start | bytes 131072 | tf_op jit(solution)/shard_map/psum | solution.py:106
Sparse Core Ops, SparseCore 0:
  90.2 143.4 all-reduce.1
where the time goes:
time: 257 us; the launch traced here: 256 us
  waiting for transfers between devices  162 us (63%)
  starting transfers between devices  37.3 us (15%)
  other arithmetic  21.4 us (8%)
  local copies, waits for them, and re-layouts  16.3 us (6%)
  between operations  14.7 us (6%)
  matrix products  4.08 us (2%)
    psum x1, waiting for transfers between devices, local(): gram_whole = lax.psum(gram_local, ('wide', 'narrow'))  144 us
    ppermute x8, starting transfers between devices, extended(): lax.ppermute(lax.slice_in_dim(block, 0, width, axis=dim), axis, backward)  23.8 us
    ppermute x8, waiting for transfers between devices, extended(): lax.ppermute(lax.slice_in_dim(block, block.shape[dim] - width, None, axis...  13.9 us
    another operation x3, other arithmetic, local(): factor = jnp.linalg.cholesky(gram_whole).T  12.4 us
    ppermute x8, starting transfers between devices, extended(): lax.ppermute(lax.slice_in_dim(block, block.shape[dim] - width, None, axis...  9.89 us
    unnamed x16, local copies, waits for them, and re-layouts  9.47 us
  transfers between devices with their start and end apart: 18, of which 14 were waited for; matrix products, arithmetic and copies ran while one was open for 5% of the time, Pallas kernels for 0%

commit v1 on v0

--- a/solution.py
+++ b/solution.py
@@ -103,7 +103,7 @@
         0,
     )
     gram_local = gram_local * inverse_cells
-    gram_whole = lax.psum(gram_local, ("wide", "narrow"))
+    gram_whole = jnp.sum(lax.all_gather(gram_local, ("wide", "narrow")), axis=0)
     factor = jnp.linalg.cholesky(gram_whole).T
     return (current, factor)
 

time: 257 us -> 429 us (1.67)
  waiting for transfers between devices: 162 us -> 332 us
    all_gather x0 -> x1, waiting for transfers between devices: none -> 314 us  [local(): gram_whole = jnp.sum(lax.all_gather(gram_local, ('wide', 'narrow')), axis=0)]
    psum x1 -> x0, waiting for transfers between devices: 144 us -> none  [local(): gram_whole = lax.psum(gram_local, ('wide', 'narrow'))]
  transfers between devices with their start and end apart: 18 -> 18, of which waited for: 14 -> 14; matrix products, arithmetic and copies ran while one was open for 5% -> 3% of each run, Pallas kernels for 0% -> 0%
where the time goes in v1:
time: 429 us; the launch traced here: 428 us
  waiting for transfers between devices  332 us (77%)
  starting transfers between devices  37.3 us (9%)
  other arithmetic  23.7 us (6%)
  local copies, waits for them, and re-layouts  16.1 us (4%)
  between operations  14.7 us (3%)
    all_gather x1, waiting for transfers between devices, local(): gram_whole = jnp.sum(lax.all_gather(gram_local, ('wide', 'narrow')), axis=0)  314 us
    ppermute x8, starting transfers between devices, extended(): lax.ppermute(lax.slice_in_dim(block, 0, width, axis=dim), axis, backward)  23.8 us
    ppermute x8, waiting for transfers between devices, extended(): lax.ppermute(lax.slice_in_dim(block, block.shape[dim] - width, None, axis...  13.9 us
    another operation x3, other arithmetic, local(): factor = jnp.linalg.cholesky(gram_whole).T  12.4 us
    ppermute x8, starting transfers between devices, extended(): lax.ppermute(lax.slice_in_dim(block, block.shape[dim] - width, None, axis...  9.89 us
    unnamed x16, local copies, waits for them, and re-layouts  9.4 us
  transfers between devices with their start and end apart: 18, of which 14 were waited for; matrix products, arithmetic and copies ran while one was open for 3% of the time, Pallas kernels for 0%

profile of v1, /device:TPU:1, one launch (start us, length us, event | category | flops | bytes accessed | tf_op | source)
XLA Modules:
  0.0 428.2 jit_solution(15845789211913904846)
XLA Ops:
  7.9 1.4 collective-permute-start.1
  9.3 1.6 collective-permute-start
  15.7 5.2 %collective-permute-start.3 = (bf16[5,3,1,256]{3,1,2,0:T(4,128)(2,1)S(1)}, bf16[5,3,1,256]{3,1,2,0:T(4,128)(2,1)S(1)}, u32[]{:S(2)}, u32[]{:S(2)}) collective-permute-start(bf16[5,3,1,256]{3,1,2,0:T(4,128)(2,1)S(1)} %copy.431), channel_id=1, source_target_pairs={{1,0},{2,1},{3,2},{4,3},{5,4},{6,5},{7,6},{0,7},{9,8},{10,9},{11,1... | collective-permute-start | bytes 23048 | tf_op jit(solution)/shard_map/ppermute | solution.py:21
  21.7 5.3 %collective-permute-done.2 = bf16[5,3,1,256]{3,1,2,0:T(4,128)(2,1)S(1)} collective-permute-done((bf16[5,3,1,256]{3,1,2,0:T(4,128)(2,1)S(1)}, bf16[5,3,1,256]{3,1,2,0:T(4,128)(2,1)S(1)}, u32[]{:S(2)}, u32[]{:S(2)}) %collective-permute-start.2) | collective-permute-done | bytes 7712 | tf_op jit(solution)/shard_map/ppermute | solution.py:18
  28.2 4.9 %collective-permute-start.5 = (bf16[5,1,8,256]{3,2,0,1:T(8,128)(2,1)S(1)}, bf16[5,1,8,256]{3,2,0,1:T(8,128)(2,1)S(1)}, u32[]{:S(2)}, u32[]{:S(2)}) collective-permute-start(bf16[5,1,8,256]{3,2,0,1:T(8,128)(2,1)S(1)} %get-tuple-element.65), channel_id=1, source_target_pairs={{8,0},{16,8},{24,16},{32,24},{40,32},{48,40},{56,48},{64,56},{72,6... | collective-permute-start | bytes 61448 | tf_op jit(solution)/shard_map/ppermute | solution.py:21
  35.6 2.3 collective-permute-start.6
  38.0 1.1 collective-permute-done.7
  39.1 2.6 collective-permute-done.6
  42.2 6.1 %collective-permute-start.9 = (bf16[5,1,8,256]{3,2,0,1:T(8,128)(2,1)S(1)}, bf16[5,1,8,256]{3,2,0,1:T(8,128)(2,1)S(1)}, u32[]{:S(2)}, u32[]{:S(2)}) collective-permute-start(bf16[5,1,8,256]{3,2,0,1:T(8,128)(2,1)S(1)} %fusion.78), channel_id=1, source_target_pairs={{8,0},{16,8},{24,16},{32,24},{40,32},{48,40},{56,48},{64,56},{72,6... | collective-permute-start | bytes 61448 | tf_op jit(solution)/shard_map/ppermute | solution.py:21
  49.7 3.0 collective-permute-start.10
  52.7 1.0 collective-permute-done.11
  53.7 2.2 collective-permute-done.10
  56.3 5.4 %collective-permute-start.13 = (bf16[5,1,8,256]{3,2,0,1:T(8,128)(2,1)S(1)}, bf16[5,1,8,256]{3,2,0,1:T(8,128)(2,1)S(1)}, u32[]{:S(2)}, u32[]{:S(2)}) collective-permute-start(bf16[5,1,8,256]{3,2,0,1:T(8,128)(2,1)S(1)} %get-tuple-element.31), channel_id=1, source_target_pairs={{8,0},{16,8},{24,16},{32,24},{40,32},{48,40},{56,48},{64,56},{72,6... | collective-permute-start | bytes 61448 | tf_op jit(solution)/shard_map/ppermute | solution.py:21
  63.1 3.0 collective-permute-start.14
  67.1 2.2 collective-permute-done.14
  71.1 2.0 reshape.659
  73.1 3.4 all-to-all-start
  76.7 3.4 fusion.2
  80.1 3.3 copy.423
  83.4 2.6 reshape.660
  86.0 1.8 copy.420
  90.0 313.6 %all-gather.2.cloned.1.call-done = f32[128,128,128]{2,1,0:T(8,128)} async-done(((f32[1,128,128]{2,1,0:T(8,128)}), f32[128,128,128]{2,1,0:T(8,128)}) %all-gather.2.cloned.1.call-update) | async-done | bytes 8388624 | tf_op jit(solution)/shard_map/all_gather | solution.py:106
  403.6 3.8 reduce_sum.9
  407.6 11.7 %cholesky.18 = f32[128,128]{1,0:T(8,128)S(1)} custom-call(f32[128,128]{1,0:T(8,128)S(1)} %fusion.6), custom_call_target="Cholesky" | custom-call | tf_op jit(solution)/shard_map/jit(cholesky)/cholesky | solution.py:107
  (146 shorter events, 20.7 us)
Async XLA Ops:
  7.9 7.6 %collective-permute-start.1 = (bf16[5,1,8,256]{3,2,1,0:T(8,128)(2,1)S(1)}, bf16[5,1,8,256]{3,2,1,0:T(8,128)(2,1)S(1)}, u32[]{:S(2)}, u32[]{:S(2)}) collective-permute-start(bf16[5,1,8,256]{3,2,1,0:T(8,128)(2,1)S(1)} %convert_element_type.30), channel_id=1, source_target_pairs={{8,0},{16,8},{24,16},{32,24},{40,32},{48,40},{56,48},{64,56},{72,6... | collective-permute-start | bytes 61448 | tf_op jit(solution)/shard_map/ppermute | solution.py:21
  9.3 6.3 %collective-permute-start = (bf16[5,1,8,256]{3,2,1,0:T(8,128)(2,1)S(1)}, bf16[5,1,8,256]{3,2,1,0:T(8,128)(2,1)S(1)}, u32[]{:S(2)}, u32[]{:S(2)}) collective-permute-start(bf16[5,1,8,256]{3,2,1,0:T(8,128)(2,1)S(1)} %convert_element_type.30), channel_id=1, source_target_pairs={{0,8},{8,16},{16,24},{24,32},{32,40},{40,48},{48,56},{56,64},{64,7... | collective-permute-start | bytes 61448 | tf_op jit(solution)/shard_map/ppermute | solution.py:18
  11.7 30.4 %copy-start = (f32[5,1,8,256]{3,2,1,0:T(8,128)S(1)}, f32[5,1,8,256]{3,2,1,0:T(8,128)}, u32[]{:S(2)}) copy-start(f32[5,1,8,256]{3,2,1,0:T(8,128)} %param.2) | copy-start | bytes 122884
  15.7 6.0 %collective-permute-start.3 = (bf16[5,3,1,256]{3,1,2,0:T(4,128)(2,1)S(1)}, bf16[5,3,1,256]{3,1,2,0:T(4,128)(2,1)S(1)}, u32[]{:S(2)}, u32[]{:S(2)}) collective-permute-start(bf16[5,3,1,256]{3,1,2,0:T(4,128)(2,1)S(1)} %copy.431), channel_id=1, source_target_pairs={{1,0},{2,1},{3,2},{4,3},{5,4},{6,5},{7,6},{0,7},{9,8},{10,9},{11,1... | collective-permute-start | bytes 23048 | tf_op jit(solution)/shard_map/ppermute | solution.py:21
  20.8 6.1 %collective-permute-start.2 = (bf16[5,3,1,256]{3,1,2,0:T(4,128)(2,1)S(1)}, bf16[5,3,1,256]{3,1,2,0:T(4,128)(2,1)S(1)}, u32[]{:S(2)}, u32[]{:S(2)}) collective-permute-start(bf16[5,3,1,256]{3,1,2,0:T(4,128)(2,1)S(1)} %copy.430), channel_id=1, source_target_pairs={{0,1},{1,2},{2,3},{3,4},{4,5},{5,6},{6,7},{7,0},{8,9},{9,10},{10,1... | collective-permute-start | bytes 23048 | tf_op jit(solution)/shard_map/ppermute | solution.py:18
  28.2 5.7 %collective-permute-start.5 = (bf16[5,1,8,256]{3,2,0,1:T(8,128)(2,1)S(1)}, bf16[5,1,8,256]{3,2,0,1:T(8,128)(2,1)S(1)}, u32[]{:S(2)}, u32[]{:S(2)}) collective-permute-start(bf16[5,1,8,256]{3,2,0,1:T(8,128)(2,1)S(1)} %get-tuple-element.65), channel_id=1, source_target_pairs={{8,0},{16,8},{24,16},{32,24},{40,32},{48,40},{56,48},{64,56},{72,6... | collective-permute-start | bytes 61448 | tf_op jit(solution)/shard_map/ppermute | solution.py:21
  33.1 1.8 collective-permute-start.4
  34.9 4.2 collective-permute-start.7
  35.6 6.1 %collective-permute-start.6 = (bf16[5,3,1,256]{3,1,2,0:T(4,128)(2,1)S(1)}, bf16[5,3,1,256]{3,1,2,0:T(4,128)(2,1)S(1)}, u32[]{:S(2)}, u32[]{:S(2)}) collective-permute-start(bf16[5,3,1,256]{3,1,2,0:T(4,128)(2,1)S(1)} %copy.385), channel_id=1, source_target_pairs={{0,1},{1,2},{2,3},{3,4},{4,5},{5,6},{6,7},{7,0},{8,9},{9,10},{10,1... | collective-permute-start | bytes 23048 | tf_op jit(solution)/shard_map/ppermute | solution.py:18
  42.2 7.0 %collective-permute-start.9 = (bf16[5,1,8,256]{3,2,0,1:T(8,128)(2,1)S(1)}, bf16[5,1,8,256]{3,2,0,1:T(8,128)(2,1)S(1)}, u32[]{:S(2)}, u32[]{:S(2)}) collective-permute-start(bf16[5,1,8,256]{3,2,0,1:T(8,128)(2,1)S(1)} %fusion.78), channel_id=1, source_target_pairs={{8,0},{16,8},{24,16},{32,24},{40,32},{48,40},{56,48},{64,56},{72,6... | collective-permute-start | bytes 61448 | tf_op jit(solution)/shard_map/ppermute | solution.py:21
  48.4 1.2 collective-permute-start.8
  49.6 4.1 collective-permute-start.11
  49.7 6.2 %collective-permute-start.10 = (bf16[5,3,1,256]{3,1,2,0:T(4,128)(2,1)S(1)}, bf16[5,3,1,256]{3,1,2,0:T(4,128)(2,1)S(1)}, u32[]{:S(2)}, u32[]{:S(2)}) collective-permute-start(bf16[5,3,1,256]{3,1,2,0:T(4,128)(2,1)S(1)} %copy.397), channel_id=1, source_target_pairs={{0,1},{1,2},{2,3},{3,4},{4,5},{5,6},{6,7},{7,0},{8,9},{9,10},{10,1... | collective-permute-start | bytes 23048 | tf_op jit(solution)/shard_map/ppermute | solution.py:18
  56.3 6.3 %collective-permute-start.13 = (bf16[5,1,8,256]{3,2,0,1:T(8,128)(2,1)S(1)}, bf16[5,1,8,256]{3,2,0,1:T(8,128)(2,1)S(1)}, u32[]{:S(2)}, u32[]{:S(2)}) collective-permute-start(bf16[5,1,8,256]{3,2,0,1:T(8,128)(2,1)S(1)} %get-tuple-element.31), channel_id=1, source_target_pairs={{8,0},{16,8},{24,16},{32,24},{40,32},{48,40},{56,48},{64,56},{72,6... | collective-permute-start | bytes 61448 | tf_op jit(solution)/shard_map/ppermute | solution.py:21
  61.8 1.2 collective-permute-start.12
  63.0 4.1 collective-permute-start.15
  63.1 6.2 %collective-permute-start.14 = (bf16[5,3,1,256]{3,1,2,0:T(4,128)(2,1)S(1)}, bf16[5,3,1,256]{3,1,2,0:T(4,128)(2,1)S(1)}, u32[]{:S(2)}, u32[]{:S(2)}) collective-permute-start(bf16[5,3,1,256]{3,1,2,0:T(4,128)(2,1)S(1)} %copy.408), channel_id=1, source_target_pairs={{0,1},{1,2},{2,3},{3,4},{4,5},{5,6},{6,7},{7,0},{8,9},{9,10},{10,1... | collective-permute-start | bytes 23048 | tf_op jit(solution)/shard_map/ppermute | solution.py:18
  73.1 10.3 %all-to-all-start = ((bf16[8,2,2560]{2,1,0:T(2,128)(2,1)}), bf16[8,2,2560]{2,1,0:T(2,128)(2,1)S(1)}, u32[]{:S(2)}, u32[]{:S(2)}) async-start(bf16[8,2,2560]{2,1,0:T(2,128)(2,1)} %reshape.659), calls=%async_computation | async-start | bytes 163840 | tf_op jit(solution)/shard_map/all_to_all | solution.py:90
  76.5 327.2 %all-gather.2.cloned.1.call-start = ((), (), s32[]{:S(2)}) async-start(), calls=%async_computation.1 | async-start | bytes 8454144 | tf_op jit(solution)/shard_map/all_gather | solution.py:106
Sparse Core Ops, SparseCore 0:
  90.1 313.4 all-gather.1
